TPU v7x, 32 devices: a whole 2x2x4 slice. The times are simulated.
32 devices in a mesh: dp: 8 (over y, x, core), tensor: 4 (over z).
Axes of the slice: x: 2, y: 2, z: 4, core: 2. Of those that a mesh axis runs over, the one named last changes fastest.
Arguments:
- inputs: bfloat16 [8, 1024, 2048], P('dp'), may hold values from -6 to 6
- segments: int32 [8, 1024], P('dp'), may hold values from 0 to 3, never falling along the last dimension, each value on 1 to 512 neighbouring positions
- cotangent: bfloat16 [8, 1024, 2048], P('dp'), may hold values from -6 to 6
- w_query: bfloat16 [2048, 2048], P(None, 'tensor'), may hold values from -0.046875 to 0.046875
- w_key: bfloat16 [2048, 2048], P(None, 'tensor'), may hold values from -0.046875 to 0.046875
- w_value: bfloat16 [2048, 2048], P(None, 'tensor'), may hold values from -0.125 to 0.125
- w_out: bfloat16 [2048, 2048], P('tensor'), may hold values from -0.5 to 0.5
- w_gate: bfloat16 [2048, 5120], P(None, 'tensor'), may hold values from -0.125 to 0.125
- w_up: bfloat16 [2048, 5120], P(None, 'tensor'), may hold values from -0.125 to 0.125
- w_down: bfloat16 [5120, 2048], P('tensor'), may hold values from -0.125 to 0.125
- gain_attn: float32 [2048], replicated, may hold values from 0.5 to 1.5
- gain_ffn: float32 [2048], replicated, may hold values from 0.5 to 1.5
- bias_table: float32 [32, 32], P(None, 'tensor'), may hold values from -4 to 4
Outputs:
- output: bfloat16 [8, 1024, 2048], P('dp', 'tensor')
- input_grad: bfloat16 [8, 1024, 2048], P('dp', 'tensor')
- query_grad: float32 [2048, 2048], P(None, 'tensor')
- key_grad: float32 [2048, 2048], P(None, 'tensor')
- value_grad: float32 [2048, 2048], P(None, 'tensor')
- out_grad: float32 [2048, 2048], P('tensor')
- gate_grad: float32 [2048, 5120], P(None, 'tensor')
- up_grad: float32 [2048, 5120], P(None, 'tensor')
- down_grad: float32 [5120, 2048], P('tensor')
- gain_attn_grad: float32 [2048], replicated
- gain_ffn_grad: float32 [2048], replicated
- table_grad: float32 [32, 32], P(None, 'tensor')
Inputs may be any that keep to these rules, and one draw needn't show every extreme that they name: `segments`: each row of 1024 tokens holds 4 documents one after another; document numbers never fall along a row; each document has 1 to 512 tokens and one in every row has exactly 512.
All inputs are finite; a program needn't handle non-finite values.
Results may differ from a plain program's by a relative error of at most 0.024.
Values may be sent and summed in bfloat16 or wider, within the bound.
A program may use at most 320 MiB of HBM per device.

v0:
```python
import jax
import jax.numpy as jnp
from jax import lax
from jax.sharding import PartitionSpec as P

thresholds = (12, 16, 23, 32, 46, 64, 91)
highest = lax.Precision.HIGHEST


def buckets_of(start_row, query_count, length):
    queries = start_row + jnp.arange(query_count, dtype=jnp.int32)
    targets = jnp.arange(length, dtype=jnp.int32)
    offset = targets[None, :] - queries[:, None]
    distance = jnp.abs(offset)
    far_bucket = jnp.full(distance.shape, 8, jnp.int32)
    for bound_value in thresholds:
        far_bucket = far_bucket + (distance >= bound_value).astype(jnp.int32)
    near_bucket = jnp.where(distance < 8, distance, far_bucket)
    return near_bucket + 16 * (offset > 0).astype(jnp.int32)


def bucket_onehot(start_row, query_count, length, bucket_count):
    bucket = buckets_of(start_row, query_count, length).reshape(1, query_count * length)
    labels = jnp.arange(bucket_count, dtype=jnp.int32)[:, None]
    return (bucket == labels).astype(jnp.float32)


def project(left_side, right_side):
    return jnp.dot(left_side, right_side, preferred_element_type=jnp.float32)


def project_back(left_side, right_side):
    return lax.dot_general(
        left_side, right_side, (((1,), (1,)), ((), ())), preferred_element_type=jnp.float32
    )


def weight_term(left_side, right_side):
    return lax.dot_general(
        left_side, right_side, (((0,), (0,)), ((), ())), preferred_element_type=jnp.float32
    )


def norm_scale(signal):
    return lax.rsqrt(jnp.mean(signal * signal, axis=-1, keepdims=True) + 1e-06)


def norm_back(signal, rms_scale, gain_vec, grad_normed):
    grad_hat = grad_normed * gain_vec
    inner_mean = jnp.mean(grad_hat * signal, axis=-1, keepdims=True)
    return rms_scale * (grad_hat - signal * rms_scale * rms_scale * inner_mean)


def gain_term(signal, rms_scale, grad_normed):
    return jnp.sum((grad_normed * signal * rms_scale).reshape(-1, signal.shape[-1]), axis=0)


def score_block(query_block, key_row, bias_block, same_doc):
    raw_scores = jnp.einsum(
        "qhd,khd->hqk", query_block, key_row, preferred_element_type=jnp.float32
    )
    return jnp.where(same_doc[None], raw_scores + bias_block, -1000000000.0)


def shards(
    inputs,
    segments,
    cotangent,
    w_query,
    w_key,
    w_value,
    w_out,
    w_gate,
    w_up,
    w_down,
    gain_attn,
    gain_ffn,
    bias_table,
):
    row_count, length, model_width = inputs.shape
    share_rows = length // lax.axis_size("tensor")
    first_row = lax.axis_index("tensor") * share_rows
    bucket_count, head_count = bias_table.shape
    local_width = w_query.shape[1]
    head_dim = local_width // head_count
    block_rows = min(512, length)
    block_count = length // block_rows
    token_count = row_count * length
    plane = (row_count, length, model_width)

    def take_share(signal):
        return lax.dynamic_slice_in_dim(signal, first_row, share_rows, 1)

    flat_inputs = inputs.reshape(token_count, model_width).astype(jnp.float32)
    scale_attn = norm_scale(flat_inputs)
    normed = (flat_inputs * scale_attn * gain_attn).astype(jnp.bfloat16)
    heads_shape = (row_count, length, head_count, head_dim)
    queries = project(normed, w_query).astype(jnp.bfloat16).reshape(heads_shape)
    key_proj = project(normed, w_key).astype(jnp.bfloat16).reshape(heads_shape)
    value_proj = project(normed, w_value).astype(jnp.bfloat16).reshape(heads_shape)
    table_heads = jnp.transpose(bias_table)
    bias_blocks = []
    for block_index in range(block_count):
        onehot = bucket_onehot(block_index * block_rows, block_rows, length, bucket_count)
        bias_flat = jnp.dot(table_heads, onehot, precision=highest)
        bias_blocks.append(bias_flat.reshape(head_count, block_rows, length))
    row_index = 0
    doc_row = segments[row_index]
    pieces = []
    totals_row = []
    for block_index in range(block_count):
        block_start = block_index * block_rows
        same_doc = doc_row[block_start : block_start + block_rows, None] == doc_row[None, :]
        query_block = queries[row_index, block_start : block_start + block_rows]
        scores = score_block(query_block, key_proj[row_index], bias_blocks[block_index], same_doc)
        row_max = jnp.max(scores, axis=-1, keepdims=True)
        weighted = jnp.exp(scores - row_max)
        row_total = jnp.sum(weighted, axis=-1, keepdims=True)
        softmaxed = (weighted / row_total).astype(jnp.bfloat16)
        totals_row.append(row_max + jnp.log(row_total))
        pieces.append(
            jnp.einsum(
                "hqk,khd->qhd", softmaxed, value_proj[row_index], preferred_element_type=jnp.float32
            ).astype(jnp.bfloat16)
        )
    log_totals = [totals_row]
    mixed_rows = [jnp.concatenate(pieces, axis=0)]
    mixed_heads = jnp.stack(mixed_rows).reshape(token_count, local_width)
    attn_part = project(mixed_heads, w_out)
    attn_total = lax.psum(attn_part.astype(jnp.bfloat16), "tensor").astype(jnp.float32)
    middle = flat_inputs + attn_total
    scale_ffn = norm_scale(middle)
    normed_ffn = (middle * scale_ffn * gain_ffn).astype(jnp.bfloat16)
    gate_pre = project(normed_ffn, w_gate)
    up_pre = project(normed_ffn, w_up)
    hidden = (jax.nn.gelu(gate_pre, approximate=True) * up_pre).astype(jnp.bfloat16)
    ffn_part = project(hidden, w_down)
    ffn_total = lax.psum(ffn_part.astype(jnp.bfloat16), "tensor").astype(jnp.float32)
    output = take_share((middle + ffn_total).reshape(plane)).astype(jnp.bfloat16)
    grad_out = cotangent.reshape(token_count, model_width)
    down_grad = weight_term(hidden, grad_out)
    grad_hidden = project_back(grad_out, w_down)
    normed_again = lax.optimization_barrier(normed_ffn)
    gate_back = project(normed_again, w_gate)
    up_back = project(normed_again, w_up)
    act_value, act_pull = jax.vjp(lambda signal: jax.nn.gelu(signal, approximate=True), gate_back)
    grad_gate = act_pull(grad_hidden * up_back)[0].astype(jnp.bfloat16)
    grad_up = (grad_hidden * act_value).astype(jnp.bfloat16)
    gate_grad = weight_term(normed_ffn, grad_gate)
    up_grad = weight_term(normed_ffn, grad_up)
    norm_ffn_part = project_back(grad_gate, w_gate) + project_back(grad_up, w_up)
    grad_normed_ffn = lax.psum(norm_ffn_part.astype(jnp.bfloat16), "tensor").astype(jnp.float32)
    grad_middle = grad_out.astype(jnp.float32) + norm_back(
        middle, scale_ffn, gain_ffn, grad_normed_ffn
    )
    gain_ffn_part = gain_term(
        take_share(middle.reshape(plane)),
        take_share(scale_ffn.reshape(row_count, length, 1)),
        take_share(grad_normed_ffn.reshape(plane)),
    )
    grad_branch = grad_middle.astype(jnp.bfloat16)
    out_grad = weight_term(mixed_heads, grad_branch)
    grad_mixed = project_back(grad_branch, w_out).astype(jnp.bfloat16).reshape(heads_shape)
    score_sums = [
        jnp.zeros((head_count, block_rows, length), jnp.float32)
        for block_index in range(block_count)
    ]
    row_index = 0
    doc_row = segments[row_index]
    key_row = key_proj[row_index]
    value_row = value_proj[row_index]
    key_sum = jnp.zeros((length, head_count, head_dim), jnp.float32)
    value_sum = jnp.zeros((length, head_count, head_dim), jnp.float32)
    query_pieces = []
    for block_index in range(block_count):
        block_start = block_index * block_rows
        same_doc = doc_row[block_start : block_start + block_rows, None] == doc_row[None, :]
        query_block = queries[row_index, block_start : block_start + block_rows]
        grad_block = grad_mixed[row_index, block_start : block_start + block_rows]
        scores = score_block(query_block, key_row, bias_blocks[block_index], same_doc)
        weights_back = jnp.exp(scores - log_totals[row_index][block_index])
        grad_weights = jnp.einsum(
            "qhd,khd->hqk", grad_block, value_row, preferred_element_type=jnp.float32
        )
        row_delta = jnp.sum(weights_back * grad_weights, axis=-1, keepdims=True)
        grad_scores = weights_back * (grad_weights - row_delta)
        score_sums[block_index] = grad_scores
        scores_low = grad_scores.astype(jnp.bfloat16)
        query_pieces.append(
            jnp.einsum(
                "hqk,khd->qhd", scores_low, key_row, preferred_element_type=jnp.float32
            ).astype(jnp.bfloat16)
        )
        key_sum = key_sum + jnp.einsum(
            "hqk,qhd->khd", scores_low, query_block, preferred_element_type=jnp.float32
        )
        value_sum = value_sum + jnp.einsum(
            "hqk,qhd->khd",
            weights_back.astype(jnp.bfloat16),
            grad_block,
            preferred_element_type=jnp.float32,
        )
    query_rows = [jnp.concatenate(query_pieces, axis=0)]
    key_rows = [key_sum.astype(jnp.bfloat16)]
    value_rows = [value_sum.astype(jnp.bfloat16)]
    grad_query = jnp.stack(query_rows).reshape(token_count, local_width)
    grad_key = jnp.stack(key_rows).reshape(token_count, local_width)
    grad_value = jnp.stack(value_rows).reshape(token_count, local_width)
    table_grad = jnp.zeros((bucket_count, head_count), jnp.float32)
    for block_index in range(block_count):
        onehot = bucket_onehot(block_index * block_rows, block_rows, length, bucket_count)
        table_grad = table_grad + lax.dot_general(
            onehot,
            score_sums[block_index].reshape(head_count, block_rows * length),
            (((1,), (1,)), ((), ())),
            precision=highest,
        )
    query_grad = weight_term(normed, grad_query)
    key_grad = weight_term(normed, grad_key)
    value_grad = weight_term(normed, grad_value)
    norm_attn_part = (
        project_back(grad_query, w_query)
        + project_back(grad_key, w_key)
        + project_back(grad_value, w_value)
    )
    grad_normed_attn = lax.psum(norm_attn_part.astype(jnp.bfloat16), "tensor").astype(jnp.float32)
    grad_input = grad_middle + norm_back(flat_inputs, scale_attn, gain_attn, grad_normed_attn)
    input_grad = take_share(grad_input.reshape(plane)).astype(jnp.bfloat16)
    gain_attn_part = gain_term(
        take_share(flat_inputs.reshape(plane)),
        take_share(scale_attn.reshape(row_count, length, 1)),
        take_share(grad_normed_attn.reshape(plane)),
    )
    gain_attn_grad, gain_ffn_grad = lax.psum((gain_attn_part, gain_ffn_part), ("dp", "tensor"))
    reduced = (
        lax.psum_scatter(
            query_grad.astype(jnp.bfloat16), "dp", scatter_dimension=0, tiled=True
        ).astype(jnp.float32),
        lax.psum_scatter(
            key_grad.astype(jnp.bfloat16), "dp", scatter_dimension=0, tiled=True
        ).astype(jnp.float32),
        lax.psum_scatter(
            value_grad.astype(jnp.bfloat16), "dp", scatter_dimension=0, tiled=True
        ).astype(jnp.float32),
        lax.psum_scatter(
            out_grad.astype(jnp.bfloat16), "dp", scatter_dimension=1, tiled=True
        ).astype(jnp.float32),
        lax.psum_scatter(
            gate_grad.astype(jnp.bfloat16), "dp", scatter_dimension=0, tiled=True
        ).astype(jnp.float32),
        lax.psum_scatter(
            up_grad.astype(jnp.bfloat16), "dp", scatter_dimension=0, tiled=True
        ).astype(jnp.float32),
        lax.psum_scatter(
            down_grad.astype(jnp.bfloat16), "dp", scatter_dimension=1, tiled=True
        ).astype(jnp.float32),
        lax.psum_scatter(
            table_grad.astype(jnp.bfloat16), "dp", scatter_dimension=0, tiled=True
        ).astype(jnp.float32),
    )
    gathered = (
        lax.all_gather(reduced[0].astype(jnp.bfloat16), "dp", axis=0, tiled=True).astype(
            jnp.float32
        ),
        lax.all_gather(reduced[1].astype(jnp.bfloat16), "dp", axis=0, tiled=True).astype(
            jnp.float32
        ),
        lax.all_gather(reduced[2].astype(jnp.bfloat16), "dp", axis=0, tiled=True).astype(
            jnp.float32
        ),
        lax.all_gather(reduced[3].astype(jnp.bfloat16), "dp", axis=1, tiled=True).astype(
            jnp.float32
        ),
        lax.all_gather(reduced[4].astype(jnp.bfloat16), "dp", axis=0, tiled=True).astype(
            jnp.float32
        ),
        lax.all_gather(reduced[5].astype(jnp.bfloat16), "dp", axis=0, tiled=True).astype(
            jnp.float32
        ),
        lax.all_gather(reduced[6].astype(jnp.bfloat16), "dp", axis=1, tiled=True).astype(
            jnp.float32
        ),
        lax.all_gather(reduced[7].astype(jnp.bfloat16), "dp", axis=0, tiled=True).astype(
            jnp.float32
        ),
    )
    return (
        output,
        input_grad,
        gathered[0],
        gathered[1],
        gathered[2],
        gathered[3],
        gathered[4],
        gathered[5],
        gathered[6],
        gain_attn_grad,
        gain_ffn_grad,
        gathered[7],
    )


def solution(mesh):
    return jax.shard_map(
        shards,
        mesh=mesh,
        in_specs=(
            P("dp", None, None),
            P("dp", None),
            P("dp", None, None),
            P(None, "tensor"),
            P(None, "tensor"),
            P(None, "tensor"),
            P("tensor", None),
            P(None, "tensor"),
            P(None, "tensor"),
            P("tensor", None),
            P(),
            P(),
            P(None, "tensor"),
        ),
        out_specs=(
            P("dp", "tensor", None),
            P("dp", "tensor", None),
            P(None, "tensor"),
            P(None, "tensor"),
            P(None, "tensor"),
            P("tensor", None),
            P(None, "tensor"),
            P(None, "tensor"),
            P("tensor", None),
            P(),
            P(),
            P(None, "tensor"),
        ),
        check_vma=False,
    )
```

profile of v0, /device:TPU:0, one launch (start us, length us, event | category | flops | bytes accessed | tf_op | source)
XLA Modules:
  0.0 1494.6 jit_solution(11549578221789818774)
XLA Ops:
  24.2 23.3 %fusion.1 = f32[524288,8]{0,1:T(8,128)} fusion(f32[32,8]{0,1:T(8,128)S(1)} %copy-done.45, s32[524288]{0:T(1024)S(1)} %fusion.51), kind=kOutput, calls=%fused_computation.2 | convolution fusion | flops 1627389952 | bytes 18875392 | tf_op jit(solution)/shard_map/dot_general | solution.py:105
  49.1 23.8 %fusion.3 = f32[524288,8]{0,1:T(8,128)} fusion(f32[32,8]{0,1:T(8,128)S(1)} %copy-done.45, s32[524288]{0:T(1024)S(1)} %fusion.50), kind=kOutput, calls=%fused_computation.5 | convolution fusion | flops 1627389952 | bytes 18875392 | tf_op jit(solution)/shard_map/dot_general | solution.py:105
  73.6 21.5 %fusion.84 = (f32[8,512]{1,0:T(8,128)S(1)}, f32[8,512,1024]{2,1,0:T(8,128)}) fusion(f32[1,8,512,1024]{3,1,2,0:T(8,128)} %bitcast.182, bf16[1024,8,64]{0,2,1:T(8,128)(2,1)S(1)} %bitcast.183, bf16[1,1024,8,64]{1,3,2,0:T(8,128)(2,1)S(1)} %bitcast.193, pred[512,1024]{1,0:T(8,128)(4,1)S(1)} %get-tuple-element.52), kind=kOutput, calls=%fused_computation.152 | convolution fusion | flops 549449728 | bytes 35667968 | tf_op jit(solution)/shard_map/qhd,khd->hqk/dot_general | solution.py:59
  95.1 7.8 fusion.11
  109.6 21.5 %fusion.85 = (f32[8,512]{1,0:T(8,128)S(1)}, f32[8,512,1024]{2,1,0:T(8,128)}) fusion(f32[1,8,512,1024]{3,1,2,0:T(8,128)} %bitcast.181, bf16[1024,8,64]{0,2,1:T(8,128)(2,1)S(1)} %bitcast.184, bf16[1,1024,8,64]{1,3,2,0:T(8,128)(2,1)S(1)} %bitcast.194, pred[512,1024]{1,0:T(8,128)(4,1)S(1)} %get-tuple-element.51), kind=kOutput, calls=%fused_computation.153 | convolution fusion | flops 549449728 | bytes 35667968 | tf_op jit(solution)/shard_map/qhd,khd->hqk/dot_general | solution.py:59
  131.1 7.8 fusion.10
  151.5 157.4 %all-reduce.7.cloned.1.call-done = bf16[1024,2048]{1,0:T(8,128)(2,1)} async-done(((bf16[1024,2048]{1,0:T(8,128)(2,1)}), bf16[1024,2048]{1,0:T(8,128)(2,1)}) %all-reduce.7.cloned.1.call-update) | async-done | bytes 4194320 | tf_op jit(solution)/shard_map/psum | solution.py:130
  317.7 7.3 fusion.87
  324.9 11.4 multiply_convert_fusion.2
  336.4 13.3 fusion.32
  349.6 7.8 fusion.88
  357.5 11.2 add_convert_fusion.1
  368.8 154.1 %all-reduce.9.cloned.1.call-done = bf16[1024,2048]{1,0:T(8,128)(2,1)} async-done(((bf16[1024,2048]{1,0:T(8,128)(2,1)}), bf16[1024,2048]{1,0:T(8,128)(2,1)}) %all-reduce.9.cloned.1.call-update) | async-done | bytes 4194320 | tf_op jit(solution)/shard_map/psum | solution.py:152
  522.8 6.7 multiply_reduce_fusion.2
  531.1 10.1 multiply_add_fusion
  541.2 6.9 fusion.64
  548.1 13.4 multiply_reduce_fusion.1
  565.7 8.8 add_convert_fusion.2
  580.0 18.7 %fusion.42 = (f32[1,8,512,1024]{3,2,1,0:T(8,128)}, bf16[8,512,1024]{2,1,0:T(8,128)(2,1)S(1)}) fusion(f32[8,512,1024]{2,1,0:T(8,128)} %get-tuple-element.68, f32[8,512]{1,0:T(8,128)S(1)} %get-tuple-element.67, f32[8,512,1024]{2,1,0:T(8,128)} %get-tuple-element.62, f32[8,512]{1,0:T(8,128)S(1)} %log_add_fusion.1), kind=kLoop, calls=%fused_computation.75 | loop fusion | flops 16777216 | bytes 58753024
  602.0 7.1 convolution_convert_fusion.5
  609.1 11.9 multiply_reduce_fusion
  621.0 19.4 %fusion.44 = (f32[1,8,512,1024]{3,2,1,0:T(8,128)}, bf16[8,512,1024]{2,1,0:T(8,128)(2,1)S(1)}) fusion(f32[8,512,1024]{2,1,0:T(8,128)} %get-tuple-element.66, f32[8,512]{1,0:T(8,128)S(1)} %get-tuple-element.65, f32[8,512,1024]{2,1,0:T(8,128)} %get-tuple-element.60, f32[8,512]{1,0:T(8,128)S(1)} %log_add_fusion), kind=kLoop, calls=%fused_computation.77 | loop fusion | flops 16777216 | bytes 58753024
  663.5 10.0 convolution_convert_fusion.2
  673.5 9.9 convolution_convert_fusion.1
  683.5 9.0 fusion.86
  692.6 9.1 fusion.41
  703.2 7.5 convolution_convert_fusion
  712.7 42.1 %reduce-scatter.8.cloned.1.call-done = bf16[256,512]{1,0:T(8,128)(2,1)} async-done(((bf16[2048,512]{1,0:T(8,128)(2,1)}), bf16[256,512]{1,0:T(8,128)(2,1)}) %reduce-scatter.8.cloned.1.call-update) | async-done | bytes 262160 | tf_op jit(solution)/shard_map/reduce_scatter | solution.py:236
  754.9 10.4 convolution_convert_fusion.3
  776.5 38.9 %reduce-scatter.16.cloned.1.call-done = bf16[256,1280]{1,0:T(8,128)(2,1)} async-done(((bf16[2048,1280]{1,0:T(8,128)(2,1)}), bf16[256,1280]{1,0:T(8,128)(2,1)}) %reduce-scatter.16.cloned.1.call-update) | async-done | bytes 655376 | tf_op jit(solution)/shard_map/reduce_scatter | solution.py:248
  815.4 60.3 %reduce-scatter.18.cloned.1.call-done = bf16[256,1280]{1,0:T(8,128)(2,1)} async-done(((bf16[2048,1280]{1,0:T(8,128)(2,1)}), bf16[256,1280]{1,0:T(8,128)(2,1)}) %reduce-scatter.18.cloned.1.call-update) | async-done | bytes 655376 | tf_op jit(solution)/shard_map/reduce_scatter | solution.py:251
  875.8 59.9 %reduce-scatter.20.cloned.1.call-done = bf16[1280,256]{1,0:T(8,128)(2,1)} async-done(((bf16[1280,2048]{1,0:T(8,128)(2,1)}), bf16[1280,256]{1,0:T(8,128)(2,1)}) %reduce-scatter.20.cloned.1.call-update) | async-done | bytes 655376 | tf_op jit(solution)/shard_map/reduce_scatter | solution.py:254
  935.8 6.7 convert_element_type.351
  944.5 18.4 %copy.33 = f32[1,8,512,1024]{3,1,2,0:T(8,128)} copy(f32[1,8,512,1024]{3,2,1,0:T(8,128)} %get-tuple-element.40) | data formatting | bytes 33554432
  962.9 18.1 %copy.34 = f32[1,8,512,1024]{3,1,2,0:T(8,128)} copy(f32[1,8,512,1024]{3,2,1,0:T(8,128)} %get-tuple-element.42) | data formatting | bytes 33554432
  981.0 34.5 %fusion = f32[32,8]{1,0:T(8,128)S(1)} fusion(f32[8,524288]{1,0:T(8,128)} %bitcast.188, s32[524288]{0:T(1024)S(1)} %copy-done.21), kind=kOutput, calls=%fused_computation.1 | convolution fusion | flops 1627389952 | bytes 18875392 | tf_op jit(solution)/shard_map/dot_general | solution.py:212
  1015.5 34.6 %fusion.74 = bf16[32,8]{1,0:T(8,128)(2,1)S(1)} fusion(f32[32,8]{1,0:T(8,128)S(1)} %fusion, f32[8,524288]{1,0:T(8,128)} %bitcast.187, s32[524288]{0:T(1024)S(1)} %copy-done.23), kind=kOutput, calls=%fused_computation.129 | convolution fusion | flops 1627390464 | bytes 18875904 | tf_op jit(solution)/shard_map/dot_general | solution.py:212
  1050.2 12.6 all-reduce
  1062.9 9.7 all-gather
  1096.6 253.2 %all-reduce.11.cloned.1.call-done = (bf16[1024,2048]{1,0:T(8,128)(2,1)}, bf16[1024,2048]{1,0:T(8,128)(2,1)}) async-done(((bf16[1024,2048]{1,0:T(8,128)(2,1)}, bf16[1024,2048]{1,0:T(8,128)(2,1)}), (bf16[1024,2048]{1,0:T(8,128)(2,1)}, bf16[1024,2048]{1,0:T(8,128)(2,1)})) %all-reduce.11.cloned.1.call-update) | async-done | bytes 8388624 | tf_op jit(solution)/shard_map/psum | solution.py:138
  1354.6 7.1 fusion.21
  1361.7 6.8 fusion.56
  1368.6 39.7 %all-reduce.1 = (f32[2048]{0:T(1024)}, f32[2048]{0:T(1024)}) all-reduce(f32[2048]{0:T(1024)S(1)} %get-tuple-element.57, f32[2048]{0:T(1024)S(1)} %get-tuple-element.70), channel_id=1, replica_groups=mesh['dp'=8,'tensor'=4] {'dp','tensor'}, use_global_device_ids=true, to_apply=%region_22.23 | all-reduce | flops 4096 | bytes 32768 | tf_op jit(solution)/shard_map/psum | solution.py:234
  1408.2 7.4 convert_element_type.419
  1415.6 20.0 %all-gather.19.cloned.1.call-done = bf16[2048,1280]{1,0:T(8,128)(2,1)} async-done(((bf16[256,1280]{1,0:T(8,128)(2,1)}), bf16[2048,1280]{1,0:T(8,128)(2,1)}) %all-gather.19.cloned.1.call-update) | async-done | bytes 5242896 | tf_op jit(solution)/shard_map/all_gather | solution.py:277
  1435.6 7.5 convert_element_type.421
  1443.2 36.4 %all-gather.21.cloned.1.call-done = bf16[1280,2048]{1,0:T(8,128)(2,1)} async-done(((bf16[1280,256]{1,0:T(8,128)(2,1)}), bf16[1280,2048]{1,0:T(8,128)(2,1)}) %all-gather.21.cloned.1.call-update) | async-done | bytes 5242896 | tf_op jit(solution)/shard_map/all_gather | solution.py:280
  1479.6 8.0 convert_element_type.423
  (220 shorter events, 129.7 us)
Async XLA Ops:
  7.2 139.4 %copy-start = (bf16[512,2048]{1,0:T(8,128)(2,1)S(1)}, bf16[512,2048]{1,0:T(8,128)(2,1)}, u32[]{:S(2)}) copy-start(bf16[512,2048]{1,0:T(8,128)(2,1)} %param.19) | copy-start | bytes 6291460
  7.2 301.7 %all-reduce.7.cloned.1.call-start = ((), (), s32[]{:S(2)}) async-start(), calls=%async_computation.7 | async-start | bytes 8388608 | tf_op jit(solution)/shard_map/psum | solution.py:130
  13.1 96.5 %copy-start.24 = (bf16[1024,512]{0,1:T(8,128)(2,1)}, bf16[1024,512]{0,1:T(8,128)(2,1)S(1)}, u32[]{:S(2)}) copy-start(bf16[1024,512]{0,1:T(8,128)(2,1)S(1)} %convolution_convert_fusion.10) | copy-start | bytes 3145732
  15.7 93.9 %copy-start.17 = (bf16[1024,512]{0,1:T(8,128)(2,1)}, bf16[1024,512]{0,1:T(8,128)(2,1)S(1)}, u32[]{:S(2)}) copy-start(bf16[1024,512]{0,1:T(8,128)(2,1)S(1)} %convolution_convert_fusion.9) | copy-start | bytes 3145732
  24.2 23.3 %copy-start.20 = (s32[524288]{0:T(1024)}, s32[524288]{0:T(1024)S(1)}, u32[]{:S(2)}) copy-start(s32[524288]{0:T(1024)S(1)} %fusion.51) | copy-start | bytes 6291460
  49.1 23.8 %copy-start.22 = (s32[524288]{0:T(1024)}, s32[524288]{0:T(1024)S(1)}, u32[]{:S(2)}) copy-start(s32[524288]{0:T(1024)S(1)} %fusion.50) | copy-start | bytes 6291460
  73.6 29.4 %copy-start.30 = (bf16[1024,512]{0,1:T(8,128)(2,1)S(1)}, bf16[1024,512]{0,1:T(8,128)(2,1)}, u32[]{:S(2)}) copy-start(bf16[1024,512]{0,1:T(8,128)(2,1)} %convolution_convert_fusion.11) | copy-start | bytes 3145732
  95.1 10.6 copy-start.2
  131.0 10.6 copy-start.3
  151.0 162.9 %copy-start.40 = (f32[2048]{0:T(1024)S(1)}, f32[2048]{0:T(1024)}, u32[]{:S(2)}) copy-start(f32[2048]{0:T(1024)} %param.24) | copy-start | bytes 24580
  151.1 371.8 %all-reduce.9.cloned.1.call-start = ((), (), s32[]{:S(2)}) async-start(), calls=%async_computation.8 | async-start | bytes 8388608 | tf_op jit(solution)/shard_map/psum | solution.py:152
  308.9 8.7 slice-start.4
  314.8 214.8 %copy-start.41 = (f32[1024]{0:T(1024)}, f32[1024]{0:T(1024)S(1)}, u32[]{:S(2)}) copy-start(f32[1024]{0:T(1024)S(1)} %add_rsqrt_fusion) | copy-start | bytes 12292
  317.6 18.7 %copy-start.26 = (bf16[1024,2048]{1,0:T(8,128)(2,1)}, bf16[1024,2048]{1,0:T(8,128)(2,1)S(1)}, u32[]{:S(2)}) copy-start(bf16[1024,2048]{1,0:T(8,128)(2,1)S(1)} %multiply_convert_fusion) | copy-start | bytes 12582916
  317.6 7.3 copy-start.31
  336.4 21.1 %copy-start.54 = (bf16[1024,1280]{1,0:T(8,128)(2,1)}, bf16[1024,1280]{1,0:T(8,128)(2,1)S(1)}, u32[]{:S(2)}) copy-start(bf16[1024,1280]{1,0:T(8,128)(2,1)S(1)} %get-tuple-element.63) | copy-start | bytes 7864324
  349.6 7.9 copy-start.55
  368.7 342.1 %reduce-scatter.12.cloned.1.call-start = ((), (), s32[]{:S(2)}) async-start(), calls=%async_computation.13 | async-start | bytes 2359296 | tf_op jit(solution)/shard_map/reduce_scatter | solution.py:242
  522.8 8.3 copy-start.16
  541.2 20.2 %slice-start = ((s8[16777216]{0:T(1024)(128)(4,1)}), s8[4194304]{0:T(1024)(128)(4,1)S(1)}, s32[]{:S(2)}) async-start(s8[16777216]{0:T(1024)(128)(4,1)} %bitcast.179), calls=%async_computation.24 | async-start | bytes 8388608
  541.2 20.2 %slice-start.1 = ((s8[16777216]{0:T(1024)(128)(4,1)}), s8[4194304]{0:T(1024)(128)(4,1)S(1)}, s32[]{:S(2)}) async-start(s8[16777216]{0:T(1024)(128)(4,1)} %bitcast.179), calls=%async_computation.25 | async-start | bytes 8388608
  548.1 13.4 slice-start.2
  548.1 13.4 slice-start.3
  565.7 9.9 copy-start.7
  565.7 9.9 copy-start.43
  565.7 9.8 copy-start.47
  579.9 131.4 %reduce-scatter.14.cloned.1.call-start = ((), (), s32[]{:S(2)}) async-start(), calls=%async_computation.15 | async-start | bytes 2359296 | tf_op jit(solution)/shard_map/reduce_scatter | solution.py:245
  580.0 18.7 %copy-start.25 = (bf16[1024,512]{0,1:T(8,128)(2,1)S(1)}, bf16[1024,512]{0,1:T(8,128)(2,1)}, u32[]{:S(2)}) copy-start(bf16[1024,512]{0,1:T(8,128)(2,1)} %copy-done.24) | copy-start | bytes 3145732
  621.0 91.1 %reduce-scatter.10.cloned.1.call-start = ((), (), s32[]{:S(2)}) async-start(), calls=%async_computation.11 | async-start | bytes 2359296 | tf_op jit(solution)/shard_map/reduce_scatter | solution.py:239
  650.0 104.8 %reduce-scatter.8.cloned.1.call-start = ((), (), s32[]{:S(2)}) async-start(), calls=%async_computation.9 | async-start | bytes 2359296 | tf_op jit(solution)/shard_map/reduce_scatter | solution.py:236
  663.4 151.9 %reduce-scatter.16.cloned.1.call-start = ((), (), s32[]{:S(2)}) async-start(), calls=%async_computation.17 | async-start | bytes 5898240 | tf_op jit(solution)/shard_map/reduce_scatter | solution.py:248
  673.5 202.2 %reduce-scatter.18.cloned.1.call-start = ((), (), s32[]{:S(2)}) async-start(), calls=%async_computation.19 | async-start | bytes 5898240 | tf_op jit(solution)/shard_map/reduce_scatter | solution.py:251
  683.5 252.3 %reduce-scatter.20.cloned.1.call-start = ((), (), s32[]{:S(2)}) async-start(), calls=%async_computation.21 | async-start | bytes 5898240 | tf_op jit(solution)/shard_map/reduce_scatter | solution.py:254
  683.5 9.1 copy-start.27
  692.6 10.6 copy-start.32
  710.7 369.1 %all-gather.13.cloned.1.call-start = ((), (), s32[]{:S(2)}) async-start(), calls=%async_computation.14 | async-start | bytes 2359296 | tf_op jit(solution)/shard_map/all_gather | solution.py:268
  711.3 372.7 %all-gather.15.cloned.1.call-start = ((), (), s32[]{:S(2)}) async-start(), calls=%async_computation.16 | async-start | bytes 2359296 | tf_op jit(solution)/shard_map/all_gather | solution.py:271
  712.0 376.1 %all-gather.11.cloned.1.call-start = ((), (), s32[]{:S(2)}) async-start(), calls=%async_computation.12 | async-start | bytes 2359296 | tf_op jit(solution)/shard_map/all_gather | solution.py:265
  712.6 379.7 %all-gather.9.cloned.1.call-start = ((), (), s32[]{:S(2)}) async-start(), calls=%async_computation.10 | async-start | bytes 2359296 | tf_op jit(solution)/shard_map/all_gather | solution.py:262
  754.8 10.5 copy-start.34
  754.8 595.0 %all-reduce.11.cloned.1.call-start = ((), (), s32[]{:S(2)}) async-start(), calls=%async_computation.23 | async-start | bytes 16777216 | tf_op jit(solution)/shard_map/psum | solution.py:138
  754.9 10.4 copy-start.49
  776.4 631.8 %all-gather.17.cloned.1.call-start = ((), (), s32[]{:S(2)}) async-start(), calls=%async_computation.18 | async-start | bytes 5898240 | tf_op jit(solution)/shard_map/all_gather | solution.py:274
  815.4 620.2 %all-gather.19.cloned.1.call-start = ((), (), s32[]{:S(2)}) async-start(), calls=%async_computation.20 | async-start | bytes 5898240 | tf_op jit(solution)/shard_map/all_gather | solution.py:277
  875.7 603.9 %all-gather.21.cloned.1.call-start = ((), (), s32[]{:S(2)}) async-start(), calls=%async_computation.22 | async-start | bytes 5898240 | tf_op jit(solution)/shard_map/all_gather | solution.py:280
  962.9 18.1 %copy-start.21 = (s32[524288]{0:T(1024)S(1)}, s32[524288]{0:T(1024)}, u32[]{:S(2)}) copy-start(s32[524288]{0:T(1024)} %copy-done.20) | copy-start | bytes 6291460
  981.0 34.5 %copy-start.23 = (s32[524288]{0:T(1024)S(1)}, s32[524288]{0:T(1024)}, u32[]{:S(2)}) copy-start(s32[524288]{0:T(1024)} %copy-done.22) | copy-start | bytes 6291460
  1435.6 52.0 %copy-start.1 = (bf16[512,2048]{1,0:T(8,128)(2,1)S(1)}, bf16[512,2048]{1,0:T(8,128)(2,1)}, u32[]{:S(2)}) copy-start(bf16[512,2048]{1,0:T(8,128)(2,1)} %param.19) | copy-start | bytes 6291460
  (31 other events, 111.3 us)
Sparse Core Ops, SparseCore 0:
  151.2 157.6 all-reduce.6
  368.8 153.9 all-reduce.8
  580.1 40.2 reduce-scatter.11
  623.8 41.2 reduce-scatter.13
  668.2 41.2 reduce-scatter.9
  713.5 41.2 reduce-scatter.7
  758.7 56.5 reduce-scatter.15
  819.1 56.5 reduce-scatter.17
  879.1 56.5 reduce-scatter.19
  937.6 27.8 all-gather.12
  967.6 28.1 all-gather.14
  997.7 27.8 all-gather.10
  1027.7 27.9 all-gather.8
  1058.3 291.5 all-reduce.10
  1351.7 40.4 all-gather.16
  1394.1 41.4 all-gather.18
  1437.5 42.0 all-gather.20
where the time goes:
time: 1500 us; the launch traced here: 1490 us
  waiting for transfers between devices  824 us (55%)
  matrix products  375 us (25%)
  other arithmetic  155 us (10%)
  blocking collectives  62 us (4%)
  local copies, waits for them, and re-layouts  61.4 us (4%)
  between operations  15.9 us (1%)
    psum x1, waiting for transfers between devices, shards(): lax.psum(ffn_part.astype(jnp.bfloat16), 'tensor').astype(jnp.float32)  253 us
    psum x1, waiting for transfers between devices, shards(): lax.psum(attn_part.astype(jnp.bfloat16), 'tensor').astype(jnp.float32)  157 us
    psum x1, waiting for transfers between devices, shards(): lax.psum(norm_ffn_part.astype(jnp.bfloat16), 'tensor').astype(jnp.float32)  154 us
    dot_general x2, matrix products, shards(): lax.dot_general(onehot, score_sums[block_index].reshape(head_count, block...  69.2 us
    dot_general x9, matrix products, project(): return jnp.dot(left_side, right_side, preferred_element_type=jnp.float32)  62.2 us
    unnamed x133, local copies, waits for them, and re-layouts  60.4 us
    reduce_scatter x1, waiting for transfers between devices, shards(): lax.psum_scatter(up_grad.astype(jnp.bfloat16), 'dp', scatter_dimension=0,...  60.3 us
    reduce_scatter x1, waiting for transfers between devices, shards(): lax.psum_scatter(down_grad.astype(jnp.bfloat16), 'dp', scatter_dimension=...  59.9 us
  transfers between devices with their start and end apart: 17, of which 9 were waited for; matrix products, arithmetic and copies ran while one was open for 21% of the time, Pallas kernels for 0%

commit v1 on v0

--- a/solution.py
+++ b/solution.py
@@ -5,6 +5,18 @@
 
 thresholds = (12, 16, 23, 32, 46, 64, 91)
 highest = lax.Precision.HIGHEST
+
+
+def gather_by_bits(value, axis, dim):
+    ways, here = (lax.axis_size(axis), lax.axis_index(axis))
+    grown, reach = (value, 1)
+    while reach < ways:
+        theirs = lax.ppermute(grown, axis, [(d, d ^ reach) for d in range(ways)])
+        mine_first = jnp.concatenate([grown, theirs], axis=dim)
+        theirs_first = jnp.concatenate([theirs, grown], axis=dim)
+        grown = jnp.where(here & reach == 0, mine_first, theirs_first)
+        reach = 2 * reach
+    return grown
 
 
 def buckets_of(start_row, query_count, length):
@@ -277,9 +289,7 @@
         lax.all_gather(reduced[5].astype(jnp.bfloat16), "dp", axis=0, tiled=True).astype(
             jnp.float32
         ),
-        lax.all_gather(reduced[6].astype(jnp.bfloat16), "dp", axis=1, tiled=True).astype(
-            jnp.float32
-        ),
+        gather_by_bits(reduced[6].astype(jnp.bfloat16), "dp", 1).astype(jnp.float32),
         lax.all_gather(reduced[7].astype(jnp.bfloat16), "dp", axis=0, tiled=True).astype(
             jnp.float32
         ),

time: 1500 us -> 1480 us (0.987)
  waiting for transfers between devices: 824 us -> 796 us
    all_gather x1 -> x0, waiting for transfers between devices: 36.4 us -> none  [shards(): lax.all_gather(reduced[6].astype(jnp.bfloat16), 'dp', axis=1, tiled=True)]
  transfers between devices with their start and end apart: 17 -> 19, of which waited for: 9 -> 9; matrix products, arithmetic and copies ran while one was open for 21% -> 22% of each run, Pallas kernels for 0% -> 0%
where the time goes in v1:
time: 1480 us; the launch traced here: 1470 us
  waiting for transfers between devices  796 us (54%)
  matrix products  375 us (25%)
  other arithmetic  163 us (11%)
  blocking collectives  61.4 us (4%)
  local copies, waits for them, and re-layouts  60.9 us (4%)
  between operations  15.9 us (1%)
    psum x1, waiting for transfers between devices, shards(): lax.psum(ffn_part.astype(jnp.bfloat16), 'tensor').astype(jnp.float32)  258 us
    psum x1, waiting for transfers between devices, shards(): lax.psum(attn_part.astype(jnp.bfloat16), 'tensor').astype(jnp.float32)  157 us
    psum x1, waiting for transfers between devices, shards(): lax.psum(norm_ffn_part.astype(jnp.bfloat16), 'tensor').astype(jnp.float32)  154 us
    dot_general x2, matrix products, shards(): lax.dot_general(onehot, score_sums[block_index].reshape(head_count, block...  69 us
    dot_general x9, matrix products, project(): return jnp.dot(left_side, right_side, preferred_element_type=jnp.float32)  62.2 us
    reduce_scatter x1, waiting for transfers between devices, shards(): lax.psum_scatter(up_grad.astype(jnp.bfloat16), 'dp', scatter_dimension=0,...  60.9 us
    reduce_scatter x1, waiting for transfers between devices, shards(): lax.psum_scatter(down_grad.astype(jnp.bfloat16), 'dp', scatter_dimension=...  60 us
    unnamed x133, local copies, waits for them, and re-layouts  59.9 us
  transfers between devices with their start and end apart: 19, of which 9 were waited for; matrix products, arithmetic and copies ran while one was open for 22% of the time, Pallas kernels for 0%

profile of v1, /device:TPU:0, one launch (start us, length us, event | category | flops | bytes accessed | tf_op | source)
XLA Modules:
  0.0 1474.8 jit_solution(17218551931943799460)
XLA Ops:
  24.2 23.2 %fusion.1 = f32[524288,8]{0,1:T(8,128)} fusion(f32[32,8]{0,1:T(8,128)S(1)} %copy-done.45, s32[524288]{0:T(1024)S(1)} %fusion.52), kind=kOutput, calls=%fused_computation.2 | convolution fusion | flops 1627389952 | bytes 18875392 | tf_op jit(solution)/shard_map/dot_general | solution.py:117
  49.1 23.6 %fusion.3 = f32[524288,8]{0,1:T(8,128)} fusion(f32[32,8]{0,1:T(8,128)S(1)} %copy-done.45, s32[524288]{0:T(1024)S(1)} %fusion.51), kind=kOutput, calls=%fused_computation.5 | convolution fusion | flops 1627389952 | bytes 18875392 | tf_op jit(solution)/shard_map/dot_general | solution.py:117
  73.4 21.6 %fusion.85 = (f32[8,512]{1,0:T(8,128)S(1)}, f32[8,512,1024]{2,1,0:T(8,128)}) fusion(f32[1,8,512,1024]{3,1,2,0:T(8,128)} %bitcast.182, bf16[1024,8,64]{0,2,1:T(8,128)(2,1)S(1)} %bitcast.183, bf16[1,1024,8,64]{1,3,2,0:T(8,128)(2,1)S(1)} %bitcast.193, pred[512,1024]{1,0:T(8,128)(4,1)S(1)} %get-tuple-element.52), kind=kOutput, calls=%fused_computation.156 | convolution fusion | flops 549449728 | bytes 35667968 | tf_op jit(solution)/shard_map/qhd,khd->hqk/dot_general | solution.py:71
  95.0 7.8 fusion.11
  109.4 21.5 %fusion.86 = (f32[8,512]{1,0:T(8,128)S(1)}, f32[8,512,1024]{2,1,0:T(8,128)}) fusion(f32[1,8,512,1024]{3,1,2,0:T(8,128)} %bitcast.181, bf16[1024,8,64]{0,2,1:T(8,128)(2,1)S(1)} %bitcast.184, bf16[1,1024,8,64]{1,3,2,0:T(8,128)(2,1)S(1)} %bitcast.194, pred[512,1024]{1,0:T(8,128)(4,1)S(1)} %get-tuple-element.51), kind=kOutput, calls=%fused_computation.157 | convolution fusion | flops 549449728 | bytes 35667968 | tf_op jit(solution)/shard_map/qhd,khd->hqk/dot_general | solution.py:71
  130.9 7.8 fusion.10
  151.4 157.4 %all-reduce.7.cloned.1.call-done = bf16[1024,2048]{1,0:T(8,128)(2,1)} async-done(((bf16[1024,2048]{1,0:T(8,128)(2,1)}), bf16[1024,2048]{1,0:T(8,128)(2,1)}) %all-reduce.7.cloned.1.call-update) | async-done | bytes 4194320 | tf_op jit(solution)/shard_map/psum | solution.py:142
  317.6 7.3 fusion.88
  324.9 11.4 multiply_convert_fusion.2
  336.3 13.3 fusion.32
  349.6 7.8 fusion.89
  357.4 11.2 add_convert_fusion.1
  368.7 154.1 %all-reduce.9.cloned.1.call-done = bf16[1024,2048]{1,0:T(8,128)(2,1)} async-done(((bf16[1024,2048]{1,0:T(8,128)(2,1)}), bf16[1024,2048]{1,0:T(8,128)(2,1)}) %all-reduce.9.cloned.1.call-update) | async-done | bytes 4194320 | tf_op jit(solution)/shard_map/psum | solution.py:164
  522.8 6.7 multiply_reduce_fusion.2
  531.1 10.1 multiply_add_fusion
  541.2 6.9 fusion.65
  548.0 13.4 multiply_reduce_fusion.1
  565.6 8.8 add_convert_fusion.2
  579.9 18.7 %fusion.43 = (f32[1,8,512,1024]{3,2,1,0:T(8,128)}, bf16[8,512,1024]{2,1,0:T(8,128)(2,1)S(1)}) fusion(f32[8,512,1024]{2,1,0:T(8,128)} %get-tuple-element.68, f32[8,512]{1,0:T(8,128)S(1)} %get-tuple-element.67, f32[8,512,1024]{2,1,0:T(8,128)} %get-tuple-element.62, f32[8,512]{1,0:T(8,128)S(1)} %log_add_fusion.1), kind=kLoop, calls=%fused_computation.77 | loop fusion | flops 16777216 | bytes 58753024
  601.9 7.1 convolution_convert_fusion.5
  609.0 11.8 multiply_reduce_fusion
  620.9 19.4 %fusion.45 = (f32[1,8,512,1024]{3,2,1,0:T(8,128)}, bf16[8,512,1024]{2,1,0:T(8,128)(2,1)S(1)}) fusion(f32[8,512,1024]{2,1,0:T(8,128)} %get-tuple-element.66, f32[8,512]{1,0:T(8,128)S(1)} %get-tuple-element.65, f32[8,512,1024]{2,1,0:T(8,128)} %get-tuple-element.60, f32[8,512]{1,0:T(8,128)S(1)} %log_add_fusion), kind=kLoop, calls=%fused_computation.79 | loop fusion | flops 16777216 | bytes 58753024
  663.3 10.0 convolution_convert_fusion.2
  673.4 9.9 convolution_convert_fusion.1
  683.4 9.0 fusion.87
  692.5 9.1 fusion.41
  703.1 7.4 convolution_convert_fusion
  712.5 42.2 %reduce-scatter.8.cloned.1.call-done = bf16[256,512]{1,0:T(8,128)(2,1)} async-done(((bf16[2048,512]{1,0:T(8,128)(2,1)}), bf16[256,512]{1,0:T(8,128)(2,1)}) %reduce-scatter.8.cloned.1.call-update) | async-done | bytes 262160 | tf_op jit(solution)/shard_map/reduce_scatter | solution.py:248
  754.8 10.4 convolution_convert_fusion.3
  776.5 38.7 %reduce-scatter.16.cloned.1.call-done = bf16[256,1280]{1,0:T(8,128)(2,1)} async-done(((bf16[2048,1280]{1,0:T(8,128)(2,1)}), bf16[256,1280]{1,0:T(8,128)(2,1)}) %reduce-scatter.16.cloned.1.call-update) | async-done | bytes 655376 | tf_op jit(solution)/shard_map/reduce_scatter | solution.py:260
  815.3 60.9 %reduce-scatter.18.cloned.1.call-done = bf16[256,1280]{1,0:T(8,128)(2,1)} async-done(((bf16[2048,1280]{1,0:T(8,128)(2,1)}), bf16[256,1280]{1,0:T(8,128)(2,1)}) %reduce-scatter.18.cloned.1.call-update) | async-done | bytes 655376 | tf_op jit(solution)/shard_map/reduce_scatter | solution.py:263
  876.2 60.0 %reduce-scatter.20.cloned.1.call-done = bf16[1280,256]{1,0:T(8,128)(2,1)} async-done(((bf16[1280,2048]{1,0:T(8,128)(2,1)}), bf16[1280,256]{1,0:T(8,128)(2,1)}) %reduce-scatter.20.cloned.1.call-update) | async-done | bytes 655376 | tf_op jit(solution)/shard_map/reduce_scatter | solution.py:266
  941.5 6.7 convert_element_type.351
  950.3 18.2 %copy.33 = f32[1,8,512,1024]{3,1,2,0:T(8,128)} copy(f32[1,8,512,1024]{3,2,1,0:T(8,128)} %get-tuple-element.40) | data formatting | bytes 33554432
  968.5 17.7 %copy.34 = f32[1,8,512,1024]{3,1,2,0:T(8,128)} copy(f32[1,8,512,1024]{3,2,1,0:T(8,128)} %get-tuple-element.42) | data formatting | bytes 33554432
  990.5 34.5 %fusion = f32[32,8]{1,0:T(8,128)S(1)} fusion(f32[8,524288]{1,0:T(8,128)} %bitcast.188, s32[524288]{0:T(1024)S(1)} %copy-done.21), kind=kOutput, calls=%fused_computation.1 | convolution fusion | flops 1627389952 | bytes 18875392 | tf_op jit(solution)/shard_map/dot_general | solution.py:224
  1025.0 34.5 %fusion.75 = bf16[32,8]{1,0:T(8,128)(2,1)S(1)} fusion(f32[32,8]{1,0:T(8,128)S(1)} %fusion, f32[8,524288]{1,0:T(8,128)} %bitcast.187, s32[524288]{0:T(1024)S(1)} %copy-done.23), kind=kOutput, calls=%fused_computation.133 | convolution fusion | flops 1627390464 | bytes 18875904 | tf_op jit(solution)/shard_map/dot_general | solution.py:224
  1059.5 12.8 all-reduce
  1072.3 9.0 all-gather
  1082.0 6.6 convert_element_type.389
  1105.6 10.8 fusion.42
  1116.4 258.3 %all-reduce.11.cloned.1.call-done = (bf16[1024,2048]{1,0:T(8,128)(2,1)}, bf16[1024,2048]{1,0:T(8,128)(2,1)}) async-done(((bf16[1024,2048]{1,0:T(8,128)(2,1)}, bf16[1024,2048]{1,0:T(8,128)(2,1)}), (bf16[1024,2048]{1,0:T(8,128)(2,1)}, bf16[1024,2048]{1,0:T(8,128)(2,1)})) %all-reduce.11.cloned.1.call-update) | async-done | bytes 8388624 | tf_op jit(solution)/shard_map/psum | solution.py:150
  1379.4 6.9 fusion.21
  1386.4 6.8 fusion.57
  1393.2 39.6 %all-reduce.1 = (f32[2048]{0:T(1024)}, f32[2048]{0:T(1024)}) all-reduce(f32[2048]{0:T(1024)S(1)} %get-tuple-element.57, f32[2048]{0:T(1024)S(1)} %get-tuple-element.70), channel_id=1, replica_groups=mesh['dp'=8,'tensor'=4] {'dp','tensor'}, use_global_device_ids=true, to_apply=%region_22.23 | all-reduce | flops 4096 | bytes 32768 | tf_op jit(solution)/shard_map/psum | solution.py:246
  1432.8 7.5 convert_element_type.419
  1440.4 20.1 %all-gather.18.cloned.1.call-done = bf16[2048,1280]{1,0:T(8,128)(2,1)} async-done(((bf16[256,1280]{1,0:T(8,128)(2,1)}), bf16[2048,1280]{1,0:T(8,128)(2,1)}) %all-gather.18.cloned.1.call-update) | async-done | bytes 5242896 | tf_op jit(solution)/shard_map/all_gather | solution.py:289
  1460.5 7.4 convert_element_type.421
  (225 shorter events, 133.0 us)
Async XLA Ops:
  7.2 139.4 %copy-start = (bf16[512,2048]{1,0:T(8,128)(2,1)S(1)}, bf16[512,2048]{1,0:T(8,128)(2,1)}, u32[]{:S(2)}) copy-start(bf16[512,2048]{1,0:T(8,128)(2,1)} %param.19) | copy-start | bytes 6291460
  7.2 301.6 %all-reduce.7.cloned.1.call-start = ((), (), s32[]{:S(2)}) async-start(), calls=%async_computation.7 | async-start | bytes 8388608 | tf_op jit(solution)/shard_map/psum | solution.py:142
  13.1 96.3 %copy-start.24 = (bf16[1024,512]{0,1:T(8,128)(2,1)}, bf16[1024,512]{0,1:T(8,128)(2,1)S(1)}, u32[]{:S(2)}) copy-start(bf16[1024,512]{0,1:T(8,128)(2,1)S(1)} %convolution_convert_fusion.10) | copy-start | bytes 3145732
  15.7 93.7 %copy-start.17 = (bf16[1024,512]{0,1:T(8,128)(2,1)}, bf16[1024,512]{0,1:T(8,128)(2,1)S(1)}, u32[]{:S(2)}) copy-start(bf16[1024,512]{0,1:T(8,128)(2,1)S(1)} %convolution_convert_fusion.9) | copy-start | bytes 3145732
  24.2 23.3 %copy-start.20 = (s32[524288]{0:T(1024)}, s32[524288]{0:T(1024)S(1)}, u32[]{:S(2)}) copy-start(s32[524288]{0:T(1024)S(1)} %fusion.52) | copy-start | bytes 6291460
  49.1 23.6 %copy-start.22 = (s32[524288]{0:T(1024)}, s32[524288]{0:T(1024)S(1)}, u32[]{:S(2)}) copy-start(s32[524288]{0:T(1024)S(1)} %fusion.51) | copy-start | bytes 6291460
  73.4 29.4 %copy-start.30 = (bf16[1024,512]{0,1:T(8,128)(2,1)S(1)}, bf16[1024,512]{0,1:T(8,128)(2,1)}, u32[]{:S(2)}) copy-start(bf16[1024,512]{0,1:T(8,128)(2,1)} %convolution_convert_fusion.11) | copy-start | bytes 3145732
  95.0 10.6 copy-start.2
  130.9 10.6 copy-start.3
  151.0 162.9 %copy-start.40 = (f32[2048]{0:T(1024)S(1)}, f32[2048]{0:T(1024)}, u32[]{:S(2)}) copy-start(f32[2048]{0:T(1024)} %param.24) | copy-start | bytes 24580
  151.0 371.8 %all-reduce.9.cloned.1.call-start = ((), (), s32[]{:S(2)}) async-start(), calls=%async_computation.8 | async-start | bytes 8388608 | tf_op jit(solution)/shard_map/psum | solution.py:164
  308.8 8.7 slice-start.4
  314.7 214.8 %copy-start.41 = (f32[1024]{0:T(1024)}, f32[1024]{0:T(1024)S(1)}, u32[]{:S(2)}) copy-start(f32[1024]{0:T(1024)S(1)} %add_rsqrt_fusion) | copy-start | bytes 12292
  317.6 18.7 %copy-start.26 = (bf16[1024,2048]{1,0:T(8,128)(2,1)}, bf16[1024,2048]{1,0:T(8,128)(2,1)S(1)}, u32[]{:S(2)}) copy-start(bf16[1024,2048]{1,0:T(8,128)(2,1)S(1)} %multiply_convert_fusion) | copy-start | bytes 12582916
  336.3 21.1 %copy-start.54 = (bf16[1024,1280]{1,0:T(8,128)(2,1)}, bf16[1024,1280]{1,0:T(8,128)(2,1)S(1)}, u32[]{:S(2)}) copy-start(bf16[1024,1280]{1,0:T(8,128)(2,1)S(1)} %get-tuple-element.63) | copy-start | bytes 7864324
  349.5 7.9 copy-start.55
  368.6 342.0 %reduce-scatter.12.cloned.1.call-start = ((), (), s32[]{:S(2)}) async-start(), calls=%async_computation.13 | async-start | bytes 2359296 | tf_op jit(solution)/shard_map/reduce_scatter | solution.py:254
  522.8 8.3 copy-start.16
  541.2 20.2 %slice-start = ((s8[16777216]{0:T(1024)(128)(4,1)}), s8[4194304]{0:T(1024)(128)(4,1)S(1)}, s32[]{:S(2)}) async-start(s8[16777216]{0:T(1024)(128)(4,1)} %bitcast.179), calls=%async_computation.23 | async-start | bytes 8388608
  541.2 20.2 %slice-start.1 = ((s8[16777216]{0:T(1024)(128)(4,1)}), s8[4194304]{0:T(1024)(128)(4,1)S(1)}, s32[]{:S(2)}) async-start(s8[16777216]{0:T(1024)(128)(4,1)} %bitcast.179), calls=%async_computation.24 | async-start | bytes 8388608
  548.0 13.4 slice-start.2
  548.0 13.4 slice-start.3
  565.6 9.8 copy-start.7
  565.6 9.8 copy-start.43
  565.6 9.8 copy-start.47
  579.8 131.4 %reduce-scatter.14.cloned.1.call-start = ((), (), s32[]{:S(2)}) async-start(), calls=%async_computation.15 | async-start | bytes 2359296 | tf_op jit(solution)/shard_map/reduce_scatter | solution.py:257
  579.8 18.7 %copy-start.25 = (bf16[1024,512]{0,1:T(8,128)(2,1)S(1)}, bf16[1024,512]{0,1:T(8,128)(2,1)}, u32[]{:S(2)}) copy-start(bf16[1024,512]{0,1:T(8,128)(2,1)} %copy-done.24) | copy-start | bytes 3145732
  620.8 91.1 %reduce-scatter.10.cloned.1.call-start = ((), (), s32[]{:S(2)}) async-start(), calls=%async_computation.11 | async-start | bytes 2359296 | tf_op jit(solution)/shard_map/reduce_scatter | solution.py:251
  649.9 104.8 %reduce-scatter.8.cloned.1.call-start = ((), (), s32[]{:S(2)}) async-start(), calls=%async_computation.9 | async-start | bytes 2359296 | tf_op jit(solution)/shard_map/reduce_scatter | solution.py:248
  663.3 151.9 %reduce-scatter.16.cloned.1.call-start = ((), (), s32[]{:S(2)}) async-start(), calls=%async_computation.17 | async-start | bytes 5898240 | tf_op jit(solution)/shard_map/reduce_scatter | solution.py:260
  673.3 202.8 %reduce-scatter.18.cloned.1.call-start = ((), (), s32[]{:S(2)}) async-start(), calls=%async_computation.19 | async-start | bytes 5898240 | tf_op jit(solution)/shard_map/reduce_scatter | solution.py:263
  683.3 252.8 %reduce-scatter.20.cloned.1.call-start = ((), (), s32[]{:S(2)}) async-start(), calls=%async_computation.21 | async-start | bytes 5898240 | tf_op jit(solution)/shard_map/reduce_scatter | solution.py:266
  683.4 9.1 copy-start.27
  692.5 10.6 copy-start.32
  710.5 378.1 %all-gather.12.cloned.1.call-start = ((), (), s32[]{:S(2)}) async-start(), calls=%async_computation.14 | async-start | bytes 2359296 | tf_op jit(solution)/shard_map/all_gather | solution.py:280
  711.1 381.9 %all-gather.14.cloned.1.call-start = ((), (), s32[]{:S(2)}) async-start(), calls=%async_computation.16 | async-start | bytes 2359296 | tf_op jit(solution)/shard_map/all_gather | solution.py:283
  711.9 385.3 %all-gather.10.cloned.1.call-start = ((), (), s32[]{:S(2)}) async-start(), calls=%async_computation.12 | async-start | bytes 2359296 | tf_op jit(solution)/shard_map/all_gather | solution.py:277
  712.4 389.0 %all-gather.8.cloned.1.call-start = ((), (), s32[]{:S(2)}) async-start(), calls=%async_computation.10 | async-start | bytes 2359296 | tf_op jit(solution)/shard_map/all_gather | solution.py:274
  754.7 10.5 copy-start.34
  754.7 620.0 %all-reduce.11.cloned.1.call-start = ((), (), s32[]{:S(2)}) async-start(), calls=%async_computation.22 | async-start | bytes 16777216 | tf_op jit(solution)/shard_map/psum | solution.py:150
  754.8 10.4 copy-start.49
  776.5 656.4 %all-gather.16.cloned.1.call-start = ((), (), s32[]{:S(2)}) async-start(), calls=%async_computation.18 | async-start | bytes 5898240 | tf_op jit(solution)/shard_map/all_gather | solution.py:286
  815.2 645.2 %all-gather.18.cloned.1.call-start = ((), (), s32[]{:S(2)}) async-start(), calls=%async_computation.20 | async-start | bytes 5898240 | tf_op jit(solution)/shard_map/all_gather | solution.py:289
  936.2 2.3 collective-permute-start
  940.1 46.1 %collective-permute-start.1 = (bf16[1280,512]{1,0:T(8,128)(2,1)S(1)}, bf16[1280,512]{1,0:T(8,128)(2,1)}, u32[]{:S(2)}, u32[]{:S(2)}) collective-permute-start(bf16[1280,512]{1,0:T(8,128)(2,1)S(1)} %maximum_select_fusion.2), channel_id=1, source_target_pairs={{0,8},{4,12},{8,0},{12,4},{16,24},{20,28},{24,16},{28,20},{1,9},{5... | collective-permute-start | bytes 3932168 | tf_op jit(solution)/shard_map/ppermute | solution.py:14
  989.9 115.7 %collective-permute-start.2 = (bf16[1280,1024]{1,0:T(8,128)(2,1)}, bf16[1280,1024]{1,0:T(8,128)(2,1)}, u32[]{:S(2)}, u32[]{:S(2)}) collective-permute-start(bf16[1280,1024]{1,0:T(8,128)(2,1)} %maximum_select_fusion.1), channel_id=1, source_target_pairs={{0,16},{4,20},{8,24},{12,28},{16,0},{20,4},{24,8},{28,12},{1,17},{... | collective-permute-start | bytes 7864328 | tf_op jit(solution)/shard_map/ppermute | solution.py:14
  990.5 34.5 %copy-start.23 = (s32[524288]{0:T(1024)S(1)}, s32[524288]{0:T(1024)}, u32[]{:S(2)}) copy-start(s32[524288]{0:T(1024)} %copy-done.22) | copy-start | bytes 6291460
  1432.8 35.0 %copy-start.1 = (bf16[512,2048]{1,0:T(8,128)(2,1)S(1)}, bf16[512,2048]{1,0:T(8,128)(2,1)}, u32[]{:S(2)}) copy-start(bf16[512,2048]{1,0:T(8,128)(2,1)} %param.19) | copy-start | bytes 6291460
  (33 other events, 122.9 us)
Sparse Core Ops, SparseCore 0:
  151.1 157.6 all-reduce.6
  368.7 153.9 all-reduce.8
  579.9 40.2 reduce-scatter.11
  623.7 41.2 reduce-scatter.13
  668.1 41.1 reduce-scatter.9
  713.4 41.2 reduce-scatter.7
  758.6 56.5 reduce-scatter.15
  819.5 56.5 reduce-scatter.17
  879.6 56.5 reduce-scatter.19
  938.0 36.3 all-gather.11
  976.5 33.9 all-gather.13
  1012.4 36.6 all-gather.9
  1051.1 29.3 all-gather.7
  1083.1 291.5 all-reduce.10
  1376.6 40.4 all-gather.15
  1419.0 41.4 all-gather.17
